TPU v7x, 32 devices: a whole 2x2x4 slice. The times are simulated.
32 devices in a mesh: table: 8 (over z, y), helper: 4 (over x, core).
Axes of the slice: x: 2, y: 2, z: 4, core: 2. Of those that a mesh axis runs over, the one named last changes fastest.
Arguments:
- tables: bfloat16 [64, 4096, 128], P('table'), may hold values from -6 to 6
- projections: bfloat16 [64, 128, 256], P('table'), may hold values from -0.0234375 to 0.0234375
- bag_rows: int32 [64, 8, 4, 8, 16], P('table', None, 'helper'), may hold values from 0 to 4095
- bag_lengths: int32 [64, 8, 4, 8], P('table', None, 'helper'), may hold values from 1 to 16
- candidates: bfloat16 [8, 4, 2048, 256], P('table', 'helper'), may hold values from -6 to 6
- request_counts: int32 [8, 4, 8], P('table', 'helper'), may hold values from 1 to 1024, as said below
- cross_down: bfloat16 [3, 512, 128], replicated, may hold values from -0.25 to 0.25
- cross_up: bfloat16 [3, 128, 512], replicated, may hold values from -0.5 to 0.5
- cross_bias: float32 [3, 512], replicated, may hold values from -3 to 3
- layer_one: bfloat16 [512, 1024], replicated, may hold values from -0.25 to 0.25
- bias_one: float32 [1024], replicated, may hold values from -2 to 2
- layer_two: bfloat16 [1024, 512], replicated, may hold values from -0.1875 to 0.1875
- bias_two: float32 [512], replicated, may hold values from -2 to 2
- layer_three: bfloat16 [512, 256], replicated, may hold values from -0.25 to 0.25
- bias_three: float32 [256], replicated, may hold values from -2 to 2
- score_weight: bfloat16 [256], replicated, may hold values from -0.375 to 0.375
Outputs:
- scores: float32 [8, 4, 2048], P('table', 'helper')
Inputs may be any that keep to these rules, and one draw needn't show every extreme that they name: For each (a, h) the 8 counts request_counts[a, h, :] sum to at most 2048; for every a exactly one h has a sum of exactly 2048, and in that list the first request holds exactly 1024 candidates.
All inputs are finite; a program needn't handle non-finite values.
Results may differ from a plain program's by a relative error of at most 0.018.
Values may be sent and summed in bfloat16 or wider, within the bound.
A program may use at most 128 MiB of HBM per device.

v0:
```python
import jax
import jax.numpy as jnp
from jax import lax
from jax.sharding import PartitionSpec as P

BLOCK = 256


def cross_network(features, context_rows, live_slots, weights):
    (
        cross_down,
        cross_up,
        cross_bias,
        layer_one,
        bias_one,
        layer_two,
        bias_two,
        layer_three,
        bias_three,
        score_weight,
    ) = weights
    cross_input = jnp.concatenate([features, context_rows], axis=1)
    anchor = cross_input.astype(jnp.float32)
    current = anchor
    for layer_number in range(cross_down.shape[0]):
        reduced = jnp.dot(
            current.astype(jnp.bfloat16),
            cross_down[layer_number],
            preferred_element_type=jnp.float32,
        ).astype(jnp.bfloat16)
        current = (
            anchor
            * (
                jnp.dot(reduced, cross_up[layer_number], preferred_element_type=jnp.float32)
                + cross_bias[layer_number]
            )
            + current
        )
    hidden = jax.nn.relu(
        jnp.dot(current.astype(jnp.bfloat16), layer_one, preferred_element_type=jnp.float32)
        + bias_one
    ).astype(jnp.bfloat16)
    hidden = jax.nn.relu(
        jnp.dot(hidden, layer_two, preferred_element_type=jnp.float32) + bias_two
    ).astype(jnp.bfloat16)
    hidden = jax.nn.relu(
        jnp.dot(hidden, layer_three, preferred_element_type=jnp.float32) + bias_three
    ).astype(jnp.bfloat16)
    result = jnp.dot(hidden, score_weight, preferred_element_type=jnp.float32)
    return jnp.where(live_slots, result, jnp.zeros_like(result))


def context_lookup(codes, context):
    labels = jnp.arange(context.shape[0], dtype=jnp.int32)
    choose = (codes[:, None] == labels[None, :]).astype(jnp.bfloat16)
    return jnp.dot(choose, context, preferred_element_type=jnp.float32).astype(jnp.bfloat16)


def block_scores(features, codes, context, weights):
    return cross_network(features, context_lookup(codes, context), codes >= 0, weights)


def slot_codes(counts, total_slots):
    ends = jnp.cumsum(counts)
    positions = jnp.arange(total_slots, dtype=jnp.int32)
    owner = jnp.sum((positions[:, None] >= ends[None, :]).astype(jnp.int32), axis=1)
    return jnp.where(owner < counts.shape[0], owner, -1)


def pool_table(table, indices, lengths):
    table_rows = table.shape[0]
    flat_rows = indices.reshape(-1, indices.shape[-1])
    flat_lengths = lengths.reshape(-1)
    labels = jnp.arange(table_rows, dtype=jnp.int32)
    tally = jnp.zeros((flat_rows.shape[0], table_rows), jnp.float32)
    for position in range(flat_rows.shape[1]):
        chosen = jnp.where(flat_lengths > position, flat_rows[:, position], -1)
        tally = tally + (chosen[:, None] == labels[None, :]).astype(jnp.float32)
    return jnp.dot(tally.astype(jnp.bfloat16), table, preferred_element_type=jnp.float32).astype(
        jnp.bfloat16
    )


def body(
    tables,
    projections,
    bag_rows,
    bag_lengths,
    candidates,
    request_counts,
    cross_down,
    cross_up,
    cross_bias,
    layer_one,
    bias_one,
    layer_two,
    bias_two,
    layer_three,
    bias_three,
    score_weight,
):
    weights = (
        cross_down,
        cross_up,
        cross_bias,
        layer_one,
        bias_one,
        layer_two,
        bias_two,
        layer_three,
        bias_three,
        score_weight,
    )
    local_tables = tables.shape[0]
    owners = bag_rows.shape[1]
    requests = bag_rows.shape[3]
    width = projections.shape[2]
    pooled_list = []
    for table_number in range(local_tables):
        pooled_list.append(
            pool_table(tables[table_number], bag_rows[table_number], bag_lengths[table_number])
        )
    projected = jnp.stack(
        [
            jnp.dot(
                pooled_list[table_number],
                projections[table_number],
                preferred_element_type=jnp.float32,
            ).astype(jnp.bfloat16)
            for table_number in range(local_tables)
        ],
        axis=0,
    )
    projected = projected.reshape(local_tables, owners, requests, width)
    received = lax.all_to_all(projected, "table", split_axis=1, concat_axis=0, tiled=True)
    context = jnp.sum(received.astype(jnp.float32), axis=(0, 1)).astype(jnp.bfloat16)
    features = candidates[0, 0]
    total_slots = features.shape[0]
    blocks = total_slots // BLOCK
    codes = slot_codes(request_counts[0, 0], total_slots)

    def empty_block():
        return jnp.zeros((BLOCK,), jnp.float32)

    def own_block(pieces):
        block_features, block_codes = pieces
        return lax.cond(
            block_codes[0] >= 0,
            lambda: block_scores(block_features, block_codes, context, weights),
            empty_block,
        )

    scores = lax.map(
        own_block, (features.reshape(blocks, BLOCK, width), codes.reshape(blocks, BLOCK))
    )
    result = scores.reshape(total_slots)
    return result.reshape(1, 1, total_slots)


def solution(mesh):
    in_specs = (
        P("table", None, None),
        P("table", None, None),
        P("table", None, "helper", None, None),
        P("table", None, "helper", None),
        P("table", "helper", None, None),
        P("table", "helper", None),
        P(),
        P(),
        P(),
        P(),
        P(),
        P(),
        P(),
        P(),
        P(),
        P(),
    )
    out_specs = P("table", "helper", None)
    return jax.shard_map(body, mesh=mesh, in_specs=in_specs, out_specs=out_specs, check_vma=False)
```

profile of v0, /device:TPU:2, one launch (start us, length us, event | category | flops | bytes accessed | tf_op | source)
XLA Modules:
  0.0 133.1 jit_solution(14103113073700829227)
XLA Ops:
  0.0 2.2 %compare_reduce_fusion.10 = (pred[8,8]{1,0:T(8,128)(4,1)S(1)}, pred[8,8]{1,0:T(8,128)(4,1)S(1)}, pred[8,8]{1,0:T(8,128)(4,1)S(1)}, pred[8,8]{1,0:T(8,128)(4,1)S(...) fusion(s32[8,8,1,8]{3,2,1,0:T(1,128)} %param.23), kind=kLoop, calls=%fused_computation.401 | loop fusion | flops 5760 | bytes 7808 | tf_op jit(solution)/shard_map/gt | solution.py:77
  2.2 1.3 compare_reduce_fusion.11
  3.6 0.9 slice_bitcast_fusion
  28.9 4.2 %fusion.46 = bf16[8,8,8,256]{3,2,0,1:T(8,128)(2,1)} fusion(bf16[8,4096,128]{2,1,0:T(8,128)(2,1)} %param.20, s32[64]{0:T(128)S(1)} %get-tuple-element.593, s32[64]{0:T(128)S(1)} %get-tuple-element.594, s32[64]{0:T(128)S(1)} %get-tuple-element.595, s32[64]{0:T(128)S(1)} %get-tuple-element.596, s32[64]{0:T(128)S(1)} %get-tuple-element.597, ...), kind=kOutput, calls=%fused_computation.61 | convolution fusion | flops 83910656 | bytes 1155072 | tf_op jit(solution)/shard_map/dot_general | solution.py:125
  33.2 4.4 %fusion.48 = bf16[8,8,8,256]{3,2,0,1:T(8,128)(2,1)} fusion(bf16[8,8,8,256]{3,2,0,1:T(8,128)(2,1)} %fusion.46, bf16[8,4096,128]{2,1,0:T(8,128)(2,1)} %param.20, s32[64]{0:T(128)S(1)} %get-tuple-element.609, s32[64]{0:T(128)S(1)} %get-tuple-element.610, s32[64]{0:T(128)S(1)} %get-tuple-element.611, s32[64]{0:T(128)S(1)} %get-tuple-element.612, ...), kind=kOutput, calls=%fused_computation.63 | convolution fusion | flops 83910656 | bytes 1155072 | tf_op jit(solution)/shard_map/dot_general | solution.py:125
  37.5 4.2 %fusion.50 = bf16[8,8,8,256]{3,2,0,1:T(8,128)(2,1)} fusion(bf16[8,8,8,256]{3,2,0,1:T(8,128)(2,1)} %fusion.48, bf16[8,4096,128]{2,1,0:T(8,128)(2,1)} %param.20, s32[64]{0:T(128)S(1)} %get-tuple-element.625, s32[64]{0:T(128)S(1)} %get-tuple-element.626, s32[64]{0:T(128)S(1)} %get-tuple-element.627, s32[64]{0:T(128)S(1)} %get-tuple-element.628, ...), kind=kOutput, calls=%fused_computation.65 | convolution fusion | flops 83910656 | bytes 1155072 | tf_op jit(solution)/shard_map/dot_general | solution.py:125
  41.8 4.2 %fusion.52 = bf16[8,8,8,256]{3,2,0,1:T(8,128)(2,1)} fusion(bf16[8,8,8,256]{3,2,0,1:T(8,128)(2,1)} %fusion.50, bf16[8,4096,128]{2,1,0:T(8,128)(2,1)} %param.20, s32[64]{0:T(128)S(1)} %get-tuple-element.641, s32[64]{0:T(128)S(1)} %get-tuple-element.642, s32[64]{0:T(128)S(1)} %get-tuple-element.643, s32[64]{0:T(128)S(1)} %get-tuple-element.644, ...), kind=kOutput, calls=%fused_computation.67 | convolution fusion | flops 83910656 | bytes 1155072 | tf_op jit(solution)/shard_map/dot_general | solution.py:125
  46.0 4.2 %fusion.54 = bf16[8,8,8,256]{3,2,0,1:T(8,128)(2,1)} fusion(bf16[8,8,8,256]{3,2,0,1:T(8,128)(2,1)} %fusion.52, bf16[8,4096,128]{2,1,0:T(8,128)(2,1)} %param.20, s32[64]{0:T(128)S(1)} %get-tuple-element.657, s32[64]{0:T(128)S(1)} %get-tuple-element.658, s32[64]{0:T(128)S(1)} %get-tuple-element.659, s32[64]{0:T(128)S(1)} %get-tuple-element.660, ...), kind=kOutput, calls=%fused_computation.69 | convolution fusion | flops 83910656 | bytes 1155072 | tf_op jit(solution)/shard_map/dot_general | solution.py:125
  50.2 4.2 %fusion.56 = bf16[8,8,8,256]{3,2,0,1:T(8,128)(2,1)} fusion(bf16[8,8,8,256]{3,2,0,1:T(8,128)(2,1)} %fusion.54, bf16[8,4096,128]{2,1,0:T(8,128)(2,1)} %param.20, s32[64]{0:T(128)S(1)} %get-tuple-element.673, s32[64]{0:T(128)S(1)} %get-tuple-element.674, s32[64]{0:T(128)S(1)} %get-tuple-element.675, s32[64]{0:T(128)S(1)} %get-tuple-element.676, ...), kind=kOutput, calls=%fused_computation.71 | convolution fusion | flops 83910656 | bytes 1155072 | tf_op jit(solution)/shard_map/dot_general | solution.py:125
  54.4 4.3 %fusion.58 = bf16[8,8,8,256]{3,2,0,1:T(8,128)(2,1)} fusion(bf16[8,8,8,256]{3,2,0,1:T(8,128)(2,1)} %fusion.56, bf16[8,4096,128]{2,1,0:T(8,128)(2,1)} %param.20, s32[64]{0:T(128)S(1)} %get-tuple-element.689, s32[64]{0:T(128)S(1)} %get-tuple-element.690, s32[64]{0:T(128)S(1)} %get-tuple-element.691, s32[64]{0:T(128)S(1)} %get-tuple-element.692, ...), kind=kOutput, calls=%fused_computation.73 | convolution fusion | flops 83910656 | bytes 1155072 | tf_op jit(solution)/shard_map/dot_general | solution.py:125
  58.7 4.5 %fusion.60 = bf16[8,8,8,256]{3,2,0,1:T(8,128)(2,1)} fusion(bf16[8,8,8,256]{3,2,0,1:T(8,128)(2,1)} %fusion.58, bf16[8,4096,128]{2,1,0:T(8,128)(2,1)} %param.20, s32[64]{0:T(128)S(1)} %get-tuple-element.705, s32[64]{0:T(128)S(1)} %get-tuple-element.706, s32[64]{0:T(128)S(1)} %get-tuple-element.707, s32[64]{0:T(128)S(1)} %get-tuple-element.708, ...), kind=kOutput, calls=%fused_computation.75 | convolution fusion | flops 83910656 | bytes 1155072 | tf_op jit(solution)/shard_map/dot_general | solution.py:125
  63.2 5.8 %all-to-all-start = ((bf16[8,8,8,256]{3,2,0,1:T(8,128)(2,1)}), bf16[8,8,8,256]{3,2,0,1:T(8,128)(2,1)S(1)}, u32[]{:S(2)}, u32[]{:S(2)}) async-start(bf16[8,8,8,256]{3,2,0,1:T(8,128)(2,1)} %fusion.60), calls=%async_computation | async-start | bytes 524288 | tf_op jit(solution)/shard_map/all_to_all | solution.py:135
  69.1 0.5 copy.437
  69.9 8.1 %all-to-all-done = bf16[8,8,8,256]{3,2,0,1:T(8,128)(2,1)S(1)} async-done(((bf16[8,8,8,256]{3,2,0,1:T(8,128)(2,1)}), bf16[8,8,8,256]{3,2,0,1:T(8,128)(2,1)S(1)}, u32[]{:S(2)}, u32[]{:S(2)}) %all-to-all-start) | async-done | bytes 262176 | tf_op jit(solution)/shard_map/all_to_all | solution.py:135
  78.1 54.4 %while.10 = (s32[]{:T(128)}, f32[8,256]{1,0:T(8,128)S(1)}, s32[8,256]{1,0:T(8,128)S(1)}, bf16[8,256,256]{1,2,0:T(8,128)(2,1)S(1)}, bf16[8,256]{1,0:T(8,128)(2,1)...) while((s32[]{:T(128)}, f32[8,256]{1,0:T(8,128)S(1)}, ...), condition=%wide.region_6.7_spmd, body=%wide.region_3.6_spmd.sunk | while | flops 811698688 | bytes 8822575 | solution.py:153
  78.1 0.6 fusion.383
  79.4 5.4 %conditional.2 = (f32[1,256]{1,0:T(1,128)S(1)}) conditional(s32[]{:T(128)} %bitcast.417, () %tuple.437, (s32[1,256]{1,0:T(1,128)S(1)}, bf16[8,256,256]{1,2,0:T(8,128)(2,1)S(1)}, s32[]{:T(128)}, bf16[8,256]{1,0:T(8,128)(2,1)S(1)}, bf16[3,512,128]{2,1,0:T(8,128)(2,1)S(1)}, /*index=5*/bf16[3,128,512]{2,1,0:T(8,128)(2,1)S(1)}, f32[3,512]{1,0:T(4,128)S(1)}, ...), branch_computations={%region_4.4_spmd, %region_5.5_spmd} | conditional | flops 811698688 | bytes 8818188 | solution.py:147
  79.8 0.5 fusion.4
  80.3 0.5 fusion.6
  81.3 2.3 %fusion.10 = bf16[256,512]{1,0:T(8,128)(2,1)S(1)} fusion(bf16[1024,512]{1,0:T(8,128)(2,1)} %get-tuple-element.138, bf16[256,512]{0,1:T(8,128)(2,1)S(1)} %fusion.9, bf16[512,1024]{1,0:T(8,128)(2,1)} %get-tuple-element.136, f32[1024]{0:T(1024)S(1)} %get-tuple-element.137, f32[512]{0:T(512)S(1)} %get-tuple-element.139), kind=kOutput, calls=%fused_computation.15 | convolution fusion | flops 538050560 | bytes 2627584 | tf_op jit(solution)/shard_map/while/body/eval_jaxpr/cond/branch_1_fun/dot_general | solution.py:44
  83.6 1.3 fusion.13
  84.9 0.6 fusion.383
  86.2 5.4 %conditional.2 = (f32[1,256]{1,0:T(1,128)S(1)}) conditional(s32[]{:T(128)} %bitcast.417, () %tuple.437, (s32[1,256]{1,0:T(1,128)S(1)}, bf16[8,256,256]{1,2,0:T(8,128)(2,1)S(1)}, s32[]{:T(128)}, bf16[8,256]{1,0:T(8,128)(2,1)S(1)}, bf16[3,512,128]{2,1,0:T(8,128)(2,1)S(1)}, /*index=5*/bf16[3,128,512]{2,1,0:T(8,128)(2,1)S(1)}, f32[3,512]{1,0:T(4,128)S(1)}, ...), branch_computations={%region_4.4_spmd, %region_5.5_spmd} | conditional | flops 811698688 | bytes 8818188 | solution.py:147
  86.6 0.5 fusion.4
  87.1 0.5 fusion.6
  88.1 2.3 %fusion.10 = bf16[256,512]{1,0:T(8,128)(2,1)S(1)} fusion(bf16[1024,512]{1,0:T(8,128)(2,1)} %get-tuple-element.138, bf16[256,512]{0,1:T(8,128)(2,1)S(1)} %fusion.9, bf16[512,1024]{1,0:T(8,128)(2,1)} %get-tuple-element.136, f32[1024]{0:T(1024)S(1)} %get-tuple-element.137, f32[512]{0:T(512)S(1)} %get-tuple-element.139), kind=kOutput, calls=%fused_computation.15 | convolution fusion | flops 538050560 | bytes 2627584 | tf_op jit(solution)/shard_map/while/body/eval_jaxpr/cond/branch_1_fun/dot_general | solution.py:44
  90.4 1.3 fusion.13
  91.7 0.6 fusion.383
  93.0 5.4 %conditional.2 = (f32[1,256]{1,0:T(1,128)S(1)}) conditional(s32[]{:T(128)} %bitcast.417, () %tuple.437, (s32[1,256]{1,0:T(1,128)S(1)}, bf16[8,256,256]{1,2,0:T(8,128)(2,1)S(1)}, s32[]{:T(128)}, bf16[8,256]{1,0:T(8,128)(2,1)S(1)}, bf16[3,512,128]{2,1,0:T(8,128)(2,1)S(1)}, /*index=5*/bf16[3,128,512]{2,1,0:T(8,128)(2,1)S(1)}, f32[3,512]{1,0:T(4,128)S(1)}, ...), branch_computations={%region_4.4_spmd, %region_5.5_spmd} | conditional | flops 811698688 | bytes 8818188 | solution.py:147
  93.4 0.5 fusion.4
  93.9 0.5 fusion.6
  94.9 2.3 %fusion.10 = bf16[256,512]{1,0:T(8,128)(2,1)S(1)} fusion(bf16[1024,512]{1,0:T(8,128)(2,1)} %get-tuple-element.138, bf16[256,512]{0,1:T(8,128)(2,1)S(1)} %fusion.9, bf16[512,1024]{1,0:T(8,128)(2,1)} %get-tuple-element.136, f32[1024]{0:T(1024)S(1)} %get-tuple-element.137, f32[512]{0:T(512)S(1)} %get-tuple-element.139), kind=kOutput, calls=%fused_computation.15 | convolution fusion | flops 538050560 | bytes 2627584 | tf_op jit(solution)/shard_map/while/body/eval_jaxpr/cond/branch_1_fun/dot_general | solution.py:44
  97.2 1.3 fusion.13
  98.5 0.6 fusion.383
  99.8 5.4 %conditional.2 = (f32[1,256]{1,0:T(1,128)S(1)}) conditional(s32[]{:T(128)} %bitcast.417, () %tuple.437, (s32[1,256]{1,0:T(1,128)S(1)}, bf16[8,256,256]{1,2,0:T(8,128)(2,1)S(1)}, s32[]{:T(128)}, bf16[8,256]{1,0:T(8,128)(2,1)S(1)}, bf16[3,512,128]{2,1,0:T(8,128)(2,1)S(1)}, /*index=5*/bf16[3,128,512]{2,1,0:T(8,128)(2,1)S(1)}, f32[3,512]{1,0:T(4,128)S(1)}, ...), branch_computations={%region_4.4_spmd, %region_5.5_spmd} | conditional | flops 811698688 | bytes 8818188 | solution.py:147
  100.2 0.5 fusion.4
  100.7 0.5 fusion.6
  101.7 2.3 %fusion.10 = bf16[256,512]{1,0:T(8,128)(2,1)S(1)} fusion(bf16[1024,512]{1,0:T(8,128)(2,1)} %get-tuple-element.138, bf16[256,512]{0,1:T(8,128)(2,1)S(1)} %fusion.9, bf16[512,1024]{1,0:T(8,128)(2,1)} %get-tuple-element.136, f32[1024]{0:T(1024)S(1)} %get-tuple-element.137, f32[512]{0:T(512)S(1)} %get-tuple-element.139), kind=kOutput, calls=%fused_computation.15 | convolution fusion | flops 538050560 | bytes 2627584 | tf_op jit(solution)/shard_map/while/body/eval_jaxpr/cond/branch_1_fun/dot_general | solution.py:44
  104.0 1.3 fusion.13
  105.3 0.6 fusion.383
  106.6 5.4 %conditional.2 = (f32[1,256]{1,0:T(1,128)S(1)}) conditional(s32[]{:T(128)} %bitcast.417, () %tuple.437, (s32[1,256]{1,0:T(1,128)S(1)}, bf16[8,256,256]{1,2,0:T(8,128)(2,1)S(1)}, s32[]{:T(128)}, bf16[8,256]{1,0:T(8,128)(2,1)S(1)}, bf16[3,512,128]{2,1,0:T(8,128)(2,1)S(1)}, /*index=5*/bf16[3,128,512]{2,1,0:T(8,128)(2,1)S(1)}, f32[3,512]{1,0:T(4,128)S(1)}, ...), branch_computations={%region_4.4_spmd, %region_5.5_spmd} | conditional | flops 811698688 | bytes 8818188 | solution.py:147
  107.0 0.5 fusion.4
  107.5 0.5 fusion.6
  108.4 2.3 %fusion.10 = bf16[256,512]{1,0:T(8,128)(2,1)S(1)} fusion(bf16[1024,512]{1,0:T(8,128)(2,1)} %get-tuple-element.138, bf16[256,512]{0,1:T(8,128)(2,1)S(1)} %fusion.9, bf16[512,1024]{1,0:T(8,128)(2,1)} %get-tuple-element.136, f32[1024]{0:T(1024)S(1)} %get-tuple-element.137, f32[512]{0:T(512)S(1)} %get-tuple-element.139), kind=kOutput, calls=%fused_computation.15 | convolution fusion | flops 538050560 | bytes 2627584 | tf_op jit(solution)/shard_map/while/body/eval_jaxpr/cond/branch_1_fun/dot_general | solution.py:44
  110.7 1.3 fusion.13
  112.1 0.6 fusion.383
  113.4 5.4 %conditional.2 = (f32[1,256]{1,0:T(1,128)S(1)}) conditional(s32[]{:T(128)} %bitcast.417, () %tuple.437, (s32[1,256]{1,0:T(1,128)S(1)}, bf16[8,256,256]{1,2,0:T(8,128)(2,1)S(1)}, s32[]{:T(128)}, bf16[8,256]{1,0:T(8,128)(2,1)S(1)}, bf16[3,512,128]{2,1,0:T(8,128)(2,1)S(1)}, /*index=5*/bf16[3,128,512]{2,1,0:T(8,128)(2,1)S(1)}, f32[3,512]{1,0:T(4,128)S(1)}, ...), branch_computations={%region_4.4_spmd, %region_5.5_spmd} | conditional | flops 811698688 | bytes 8818188 | solution.py:147
  113.8 0.5 fusion.4
  114.2 0.5 fusion.6
  115.2 2.3 %fusion.10 = bf16[256,512]{1,0:T(8,128)(2,1)S(1)} fusion(bf16[1024,512]{1,0:T(8,128)(2,1)} %get-tuple-element.138, bf16[256,512]{0,1:T(8,128)(2,1)S(1)} %fusion.9, bf16[512,1024]{1,0:T(8,128)(2,1)} %get-tuple-element.136, f32[1024]{0:T(1024)S(1)} %get-tuple-element.137, f32[512]{0:T(512)S(1)} %get-tuple-element.139), kind=kOutput, calls=%fused_computation.15 | convolution fusion | flops 538050560 | bytes 2627584 | tf_op jit(solution)/shard_map/while/body/eval_jaxpr/cond/branch_1_fun/dot_general | solution.py:44
  117.5 1.3 fusion.13
  118.9 0.6 fusion.383
  120.2 5.4 %conditional.2 = (f32[1,256]{1,0:T(1,128)S(1)}) conditional(s32[]{:T(128)} %bitcast.417, () %tuple.437, (s32[1,256]{1,0:T(1,128)S(1)}, bf16[8,256,256]{1,2,0:T(8,128)(2,1)S(1)}, s32[]{:T(128)}, bf16[8,256]{1,0:T(8,128)(2,1)S(1)}, bf16[3,512,128]{2,1,0:T(8,128)(2,1)S(1)}, /*index=5*/bf16[3,128,512]{2,1,0:T(8,128)(2,1)S(1)}, f32[3,512]{1,0:T(4,128)S(1)}, ...), branch_computations={%region_4.4_spmd, %region_5.5_spmd} | conditional | flops 811698688 | bytes 8818188 | solution.py:147
  120.5 0.5 fusion.4
  121.0 0.5 fusion.6
  122.0 2.3 %fusion.10 = bf16[256,512]{1,0:T(8,128)(2,1)S(1)} fusion(bf16[1024,512]{1,0:T(8,128)(2,1)} %get-tuple-element.138, bf16[256,512]{0,1:T(8,128)(2,1)S(1)} %fusion.9, bf16[512,1024]{1,0:T(8,128)(2,1)} %get-tuple-element.136, f32[1024]{0:T(1024)S(1)} %get-tuple-element.137, f32[512]{0:T(512)S(1)} %get-tuple-element.139), kind=kOutput, calls=%fused_computation.15 | convolution fusion | flops 538050560 | bytes 2627584 | tf_op jit(solution)/shard_map/while/body/eval_jaxpr/cond/branch_1_fun/dot_general | solution.py:44
  124.3 1.3 fusion.13
  125.7 0.6 fusion.383
  127.0 5.4 %conditional.2 = (f32[1,256]{1,0:T(1,128)S(1)}) conditional(s32[]{:T(128)} %bitcast.417, () %tuple.437, (s32[1,256]{1,0:T(1,128)S(1)}, bf16[8,256,256]{1,2,0:T(8,128)(2,1)S(1)}, s32[]{:T(128)}, bf16[8,256]{1,0:T(8,128)(2,1)S(1)}, bf16[3,512,128]{2,1,0:T(8,128)(2,1)S(1)}, /*index=5*/bf16[3,128,512]{2,1,0:T(8,128)(2,1)S(1)}, f32[3,512]{1,0:T(4,128)S(1)}, ...), branch_computations={%region_4.4_spmd, %region_5.5_spmd} | conditional | flops 811698688 | bytes 8818188 | solution.py:147
  127.3 0.5 fusion.4
  127.8 0.5 fusion.6
  128.8 2.3 %fusion.10 = bf16[256,512]{1,0:T(8,128)(2,1)S(1)} fusion(bf16[1024,512]{1,0:T(8,128)(2,1)} %get-tuple-element.138, bf16[256,512]{0,1:T(8,128)(2,1)S(1)} %fusion.9, bf16[512,1024]{1,0:T(8,128)(2,1)} %get-tuple-element.136, f32[1024]{0:T(1024)S(1)} %get-tuple-element.137, f32[512]{0:T(512)S(1)} %get-tuple-element.139), kind=kOutput, calls=%fused_computation.15 | convolution fusion | flops 538050560 | bytes 2627584 | tf_op jit(solution)/shard_map/while/body/eval_jaxpr/cond/branch_1_fun/dot_general | solution.py:44
  131.1 1.3 fusion.13
  132.5 0.6 reshape_reshape.3
  (418 shorter events, 30.8 us)
Async XLA Ops:
  0.0 28.9 %copy-start.4 = (bf16[8,128,256]{2,1,0:T(8,128)(2,1)S(1)}, bf16[8,128,256]{2,1,0:T(8,128)(2,1)}, u32[]{:S(2)}) copy-start(bf16[8,128,256]{2,1,0:T(8,128)(2,1)} %param.21) | copy-start | bytes 1572868
  54.4 14.7 %copy-start.2 = (bf16[1,1,2048,256]{3,2,1,0:T(8,128)(2,1)S(1)}, bf16[1,1,2048,256]{3,2,1,0:T(8,128)(2,1)}, u32[]{:S(2)}) copy-start(bf16[1,1,2048,256]{3,2,1,0:T(8,128)(2,1)} %param.24) | copy-start | bytes 3145732
  54.4 15.2 %copy-start.8 = (s32[1,1,8]{2,1,0:T(1,128)S(1)}, s32[1,1,8]{2,1,0:T(1,128)}, u32[]{:S(2)}) copy-start(s32[1,1,8]{2,1,0:T(1,128)} %param.25) | copy-start | bytes 100
  58.7 19.4 %copy-start = (bf16[3,512,128]{2,1,0:T(8,128)(2,1)S(1)}, bf16[3,512,128]{2,1,0:T(8,128)(2,1)}, u32[]{:S(2)}) copy-start(bf16[3,512,128]{2,1,0:T(8,128)(2,1)} %param.26) | copy-start | bytes 1179652
  58.7 19.4 %copy-start.1 = (bf16[3,128,512]{2,1,0:T(8,128)(2,1)S(1)}, bf16[3,128,512]{2,1,0:T(8,128)(2,1)}, u32[]{:S(2)}) copy-start(bf16[3,128,512]{2,1,0:T(8,128)(2,1)} %param.27) | copy-start | bytes 1179652
  58.7 19.4 %copy-start.3 = (f32[3,512]{1,0:T(4,128)S(1)}, f32[3,512]{1,0:T(4,128)}, u32[]{:S(2)}) copy-start(f32[3,512]{1,0:T(4,128)} %param.28) | copy-start | bytes 18436
  58.7 19.4 %copy-start.5 = (f32[1024]{0:T(1024)S(1)}, f32[1024]{0:T(1024)}, u32[]{:S(2)}) copy-start(f32[1024]{0:T(1024)} %param.30) | copy-start | bytes 12292
  58.7 19.4 %copy-start.6 = (f32[512]{0:T(512)S(1)}, f32[512]{0:T(512)}, u32[]{:S(2)}) copy-start(f32[512]{0:T(512)} %param.32) | copy-start | bytes 6148
  58.7 19.4 %copy-start.7 = (f32[256]{0:T(256)S(1)}, f32[256]{0:T(256)}, u32[]{:S(2)}) copy-start(f32[256]{0:T(256)} %param.34) | copy-start | bytes 3076
  58.7 19.4 %copy-start.9 = (bf16[256]{0:T(256)(128)(2,1)S(1)}, bf16[256]{0:T(256)(128)(2,1)}, u32[]{:S(2)}) copy-start(bf16[256]{0:T(256)(128)(2,1)} %param.35) | copy-start | bytes 1540
  63.2 14.8 %all-to-all-start = ((bf16[8,8,8,256]{3,2,0,1:T(8,128)(2,1)}), bf16[8,8,8,256]{3,2,0,1:T(8,128)(2,1)S(1)}, u32[]{:S(2)}, u32[]{:S(2)}) async-start(bf16[8,8,8,256]{3,2,0,1:T(8,128)(2,1)} %fusion.60), calls=%async_computation | async-start | bytes 524288 | tf_op jit(solution)/shard_map/all_to_all | solution.py:135
where the time goes:
time: 134 us; the launch traced here: 133 us
  matrix products  76.8 us (57%)
  local copies, waits for them, and re-layouts  26 us (19%)
  other arithmetic  9.15 us (7%)
  waiting for transfers between devices  8.07 us (6%)
  loops' own time  6.45 us (5%)
  starting transfers between devices  5.83 us (4%)
    dot_general x8, matrix products, body(): jnp.dot(pooled_list[table_number], projections[table_number], preferred_e...  34.2 us
    dot_general x8, matrix products, cross_network(): jnp.dot(hidden, layer_two, preferred_element_type=jnp.float32) + bias_two  18.3 us
    gt x128, local copies, waits for them, and re-layouts, pool_table(): chosen = jnp.where(flat_lengths > position, flat_rows[:, position], -1)  12.5 us
    dot_general x24, matrix products, cross_network(): jnp.dot(reduced, cross_up[layer_number], preferred_element_type=jnp.float32)  11.7 us
    dot_general x8, matrix products, cross_network(): result = jnp.dot(hidden, score_weight, preferred_element_type=jnp.float32)  10.4 us
    unnamed x148, local copies, waits for them, and re-layouts  9.31 us
    all_to_all x1, waiting for transfers between devices, body(): lax.all_to_all(projected, 'table', split_axis=1, concat_axis=0, tiled=True)  8.07 us
    all_to_all x1, starting transfers between devices, body(): lax.all_to_all(projected, 'table', split_axis=1, concat_axis=0, tiled=True)  5.83 us
  transfers between devices with their start and end apart: 1, of which 1 were waited for; matrix products, arithmetic and copies ran while one was open for 1% of the time, Pallas kernels for 0%

commit v1 on v0

--- a/solution.py
+++ b/solution.py
@@ -132,7 +132,12 @@
         axis=0,
     )
     projected = projected.reshape(local_tables, owners, requests, width)
-    received = lax.all_to_all(projected, "table", split_axis=1, concat_axis=0, tiled=True)
+    received = jnp.concatenate(
+        lax.all_to_all(
+            jnp.stack(jnp.split(projected, lax.axis_size("table"), axis=1)), "table", 0, 0
+        ),
+        axis=0,
+    )
     context = jnp.sum(received.astype(jnp.float32), axis=(0, 1)).astype(jnp.bfloat16)
     features = candidates[0, 0]
     total_slots = features.shape[0]

time: 134 us -> 126 us (0.940)
  matrix products: 76.8 us -> 64.2 us
  local copies, waits for them, and re-layouts: 26 us -> 30.9 us
    dot_general x8, matrix products: 10.4 us -> 2.78 us  [cross_network(): result = jnp.dot(hidden, score_weight, preferred_element_type=jnp.float32)]
    dot_general x8, matrix products: 34.2 us -> 29.2 us  [body(): jnp.dot(pooled_list[table_number], projections[table_number], preferred_e...]
    unnamed x148 -> x157, local copies, waits for them, and re-layouts: 9.31 us -> 13.6 us
where the time goes in v1:
time: 126 us; the launch traced here: 125 us
  matrix products  64.2 us (51%)
  local copies, waits for them, and re-layouts  30.9 us (25%)
  other arithmetic  9.15 us (7%)
  waiting for transfers between devices  8.07 us (6%)
  loops' own time  6.45 us (5%)
  starting transfers between devices  5.83 us (5%)
    dot_general x8, matrix products, body(): jnp.dot(pooled_list[table_number], projections[table_number], preferred_e...  29.2 us
    dot_general x8, matrix products, cross_network(): jnp.dot(hidden, layer_two, preferred_element_type=jnp.float32) + bias_two  18.3 us
    unnamed x157, local copies, waits for them, and re-layouts  13.6 us
    gt x128, local copies, waits for them, and re-layouts, pool_table(): chosen = jnp.where(flat_lengths > position, flat_rows[:, position], -1)  12.5 us
    dot_general x24, matrix products, cross_network(): jnp.dot(reduced, cross_up[layer_number], preferred_element_type=jnp.float32)  11.7 us
    all_to_all x1, waiting for transfers between devices, body(): lax.all_to_all(jnp.stack(jnp.split(projected, lax.axis_size('table'), axi...  8.07 us
    all_to_all x1, starting transfers between devices, body(): lax.all_to_all(jnp.stack(jnp.split(projected, lax.axis_size('table'), axi...  5.83 us
    another operation x1, loops' own time, body(): lax.map(own_block, (features.reshape(blocks, BLOCK, width), codes.reshape...  5.8 us
  transfers between devices with their start and end apart: 1, of which 1 were waited for; matrix products, arithmetic and copies ran while one was open for 1% of the time, Pallas kernels for 0%

profile of v1, /device:TPU:2, one launch (start us, length us, event | category | flops | bytes accessed | tf_op | source)
XLA Modules:
  0.0 125.4 jit_solution(4641504969581677895)
XLA Ops:
  0.0 2.2 %compare_reduce_fusion.10 = (pred[8,8]{1,0:T(8,128)(4,1)S(1)}, pred[8,8]{1,0:T(8,128)(4,1)S(1)}, pred[8,8]{1,0:T(8,128)(4,1)S(1)}, pred[8,8]{1,0:T(8,128)(4,1)S(...) fusion(s32[8,8,1,8]{3,2,1,0:T(1,128)} %param.23), kind=kLoop, calls=%fused_computation.417 | loop fusion | flops 5760 | bytes 7808 | tf_op jit(solution)/shard_map/gt | solution.py:77
  2.2 1.3 %compare_reduce_fusion.11 = (pred[8,8]{1,0:T(8,128)(4,1)S(1)}, pred[8,8]{1,0:T(8,128)(4,1)S(1)}, pred[8,8]{1,0:T(8,128)(4,1)S(1)}, pred[8,8]{1,0:T(8,128)(4,1)S(...) fusion(s32[8,8,1,8]{3,2,1,0:T(1,128)} %param.23), kind=kLoop, calls=%fused_computation.418 | loop fusion | flops 2432 | bytes 3712 | tf_op jit(solution)/shard_map/gt | solution.py:77
  3.6 0.9 slice_bitcast_fusion.8
  28.9 3.6 %fusion.46 = bf16[8,8,8,256]{3,2,1,0:T(8,128)(2,1)S(1)} fusion(bf16[8,4096,128]{2,1,0:T(8,128)(2,1)} %param.20, s32[64]{0:T(128)S(1)} %get-tuple-element.578, s32[64]{0:T(128)S(1)} %get-tuple-element.579, s32[64]{0:T(128)S(1)} %get-tuple-element.580, s32[64]{0:T(128)S(1)} %get-tuple-element.581, s32[64]{0:T(128)S(1)} %get-tuple-element.582, ...), kind=kOutput, calls=%fused_computation.61 | convolution fusion | flops 83910656 | bytes 1155072 | tf_op jit(solution)/shard_map/dot_general | solution.py:125
  32.5 3.8 %fusion.48 = bf16[8,8,8,256]{3,2,1,0:T(8,128)(2,1)S(1)} fusion(bf16[8,8,8,256]{3,2,1,0:T(8,128)(2,1)S(1)} %fusion.46, bf16[8,4096,128]{2,1,0:T(8,128)(2,1)} %param.20, s32[64]{0:T(128)S(1)} %get-tuple-element.594, s32[64]{0:T(128)S(1)} %get-tuple-element.595, s32[64]{0:T(128)S(1)} %get-tuple-element.596, s32[64]{0:T(128)S(1)} %get-tuple-element.597, ...), kind=kOutput, calls=%fused_computation.63 | convolution fusion | flops 83910656 | bytes 1155072 | tf_op jit(solution)/shard_map/dot_general | solution.py:125
  36.3 3.6 %fusion.50 = bf16[8,8,8,256]{3,2,1,0:T(8,128)(2,1)S(1)} fusion(bf16[8,8,8,256]{3,2,1,0:T(8,128)(2,1)S(1)} %fusion.48, bf16[8,4096,128]{2,1,0:T(8,128)(2,1)} %param.20, s32[64]{0:T(128)S(1)} %get-tuple-element.610, s32[64]{0:T(128)S(1)} %get-tuple-element.611, s32[64]{0:T(128)S(1)} %get-tuple-element.612, s32[64]{0:T(128)S(1)} %get-tuple-element.613, ...), kind=kOutput, calls=%fused_computation.65 | convolution fusion | flops 83910656 | bytes 1155072 | tf_op jit(solution)/shard_map/dot_general | solution.py:125
  39.8 3.6 %fusion.52 = bf16[8,8,8,256]{3,2,1,0:T(8,128)(2,1)S(1)} fusion(bf16[8,8,8,256]{3,2,1,0:T(8,128)(2,1)S(1)} %fusion.50, bf16[8,4096,128]{2,1,0:T(8,128)(2,1)} %param.20, s32[64]{0:T(128)S(1)} %get-tuple-element.626, s32[64]{0:T(128)S(1)} %get-tuple-element.627, s32[64]{0:T(128)S(1)} %get-tuple-element.628, s32[64]{0:T(128)S(1)} %get-tuple-element.629, ...), kind=kOutput, calls=%fused_computation.67 | convolution fusion | flops 83910656 | bytes 1155072 | tf_op jit(solution)/shard_map/dot_general | solution.py:125
  43.4 3.6 %fusion.54 = bf16[8,8,8,256]{3,2,1,0:T(8,128)(2,1)S(1)} fusion(bf16[8,8,8,256]{3,2,1,0:T(8,128)(2,1)S(1)} %fusion.52, bf16[8,4096,128]{2,1,0:T(8,128)(2,1)} %param.20, s32[64]{0:T(128)S(1)} %get-tuple-element.642, s32[64]{0:T(128)S(1)} %get-tuple-element.643, s32[64]{0:T(128)S(1)} %get-tuple-element.644, s32[64]{0:T(128)S(1)} %get-tuple-element.645, ...), kind=kOutput, calls=%fused_computation.69 | convolution fusion | flops 83910656 | bytes 1155072 | tf_op jit(solution)/shard_map/dot_general | solution.py:125
  47.0 3.6 %fusion.56 = bf16[8,8,8,256]{3,2,1,0:T(8,128)(2,1)S(1)} fusion(bf16[8,8,8,256]{3,2,1,0:T(8,128)(2,1)S(1)} %fusion.54, bf16[8,4096,128]{2,1,0:T(8,128)(2,1)} %param.20, s32[64]{0:T(128)S(1)} %get-tuple-element.658, s32[64]{0:T(128)S(1)} %get-tuple-element.659, s32[64]{0:T(128)S(1)} %get-tuple-element.660, s32[64]{0:T(128)S(1)} %get-tuple-element.661, ...), kind=kOutput, calls=%fused_computation.71 | convolution fusion | flops 83910656 | bytes 1155072 | tf_op jit(solution)/shard_map/dot_general | solution.py:125
  50.6 3.7 %fusion.58 = bf16[8,8,8,256]{3,2,1,0:T(8,128)(2,1)S(1)} fusion(bf16[8,8,8,256]{3,2,1,0:T(8,128)(2,1)S(1)} %fusion.56, bf16[8,4096,128]{2,1,0:T(8,128)(2,1)} %param.20, s32[64]{0:T(128)S(1)} %get-tuple-element.674, s32[64]{0:T(128)S(1)} %get-tuple-element.675, s32[64]{0:T(128)S(1)} %get-tuple-element.676, s32[64]{0:T(128)S(1)} %get-tuple-element.677, ...), kind=kOutput, calls=%fused_computation.73 | convolution fusion | flops 83910656 | bytes 1155072 | tf_op jit(solution)/shard_map/dot_general | solution.py:125
  54.4 3.9 %fusion.60 = bf16[8,8,8,256]{3,2,1,0:T(8,128)(2,1)S(1)} fusion(bf16[8,8,8,256]{3,2,1,0:T(8,128)(2,1)S(1)} %fusion.58, bf16[8,4096,128]{2,1,0:T(8,128)(2,1)} %param.20, s32[64]{0:T(128)S(1)} %get-tuple-element.690, s32[64]{0:T(128)S(1)} %get-tuple-element.691, s32[64]{0:T(128)S(1)} %get-tuple-element.692, s32[64]{0:T(128)S(1)} %get-tuple-element.693, ...), kind=kOutput, calls=%fused_computation.75 | convolution fusion | flops 83910656 | bytes 1155072 | tf_op jit(solution)/shard_map/dot_general | solution.py:125
  58.3 0.6 constant_dynamic-update-slice_fusion.7
  58.9 0.6 constant_dynamic-update-slice_fusion.6
  59.5 0.6 constant_dynamic-update-slice_fusion.5
  60.1 0.6 constant_dynamic-update-slice_fusion.4
  60.7 0.6 constant_dynamic-update-slice_fusion.3
  61.3 0.6 constant_dynamic-update-slice_fusion.2
  61.9 0.6 constant_dynamic-update-slice_fusion.1
  62.5 0.6 constant_dynamic-update-slice_fusion
  63.1 5.8 %all-to-all-start = ((bf16[8,8,1,8,256]{4,3,1,2,0:T(8,128)(2,1)}), bf16[8,8,1,8,256]{4,3,1,2,0:T(8,128)(2,1)S(1)}, u32[]{:S(2)}, u32[]{:S(2)}) async-start(bf16[8,8,1,8,256]{4,3,1,2,0:T(8,128)(2,1)} %constant_dynamic-update-slice_fusion), calls=%async_computation | async-start | bytes 524288 | tf_op jit(solution)/shard_map/all_to_all | solution.py:136
  69.0 0.5 copy.310
  69.8 8.1 %all-to-all-done = bf16[8,8,1,8,256]{4,3,1,2,0:T(8,128)(2,1)S(1)} async-done(((bf16[8,8,1,8,256]{4,3,1,2,0:T(8,128)(2,1)}), bf16[8,8,1,8,256]{4,3,1,2,0:T(8,128)(2,1)S(1)}, u32[]{:S(2)}, u32[]{:S(2)}) %all-to-all-start) | async-done | bytes 262176 | tf_op jit(solution)/shard_map/all_to_all | solution.py:136
  78.0 46.8 %while.10 = (s32[]{:T(128)}, f32[8,256]{1,0:T(8,128)S(1)}, s32[8,256]{1,0:T(8,128)S(1)}, bf16[8,256,256]{1,2,0:T(8,128)(2,1)S(1)}, bf16[8,256]{1,0:T(8,128)(2,1)...) while((s32[]{:T(128)}, f32[8,256]{1,0:T(8,128)S(1)}, ...), condition=%wide.region_6.7_spmd, body=%wide.region_3.6_spmd.sunk | while | flops 811698688 | bytes 8822575 | solution.py:158
  78.1 0.6 fusion.383
  79.4 4.5 %conditional.2 = (f32[1,256]{1,0:T(1,128)S(1)}) conditional(s32[]{:T(128)} %bitcast.447, () %tuple.436, (s32[1,256]{1,0:T(1,128)S(1)}, bf16[8,256,256]{1,2,0:T(8,128)(2,1)S(1)}, s32[]{:T(128)}, bf16[8,256]{1,0:T(8,128)(2,1)S(1)}, bf16[3,512,128]{2,1,0:T(8,128)(2,1)S(1)}, /*index=5*/bf16[3,128,512]{2,1,0:T(8,128)(2,1)S(1)}, f32[3,512]{1,0:T(4,128)S(1)}, ...), branch_computations={%region_4.4_spmd, %region_5.5_spmd} | conditional | flops 811698688 | bytes 8818188 | solution.py:152
  79.7 0.5 fusion.4
  80.2 0.5 fusion.6
  81.2 2.3 %fusion.10 = bf16[256,512]{1,0:T(8,128)(2,1)S(1)} fusion(bf16[1024,512]{1,0:T(8,128)(2,1)} %get-tuple-element.138, bf16[256,512]{0,1:T(8,128)(2,1)S(1)} %fusion.9, bf16[512,1024]{1,0:T(8,128)(2,1)} %get-tuple-element.136, f32[1024]{0:T(1024)S(1)} %get-tuple-element.137, f32[512]{0:T(512)S(1)} %get-tuple-element.139), kind=kOutput, calls=%fused_computation.15 | convolution fusion | flops 538050560 | bytes 2627584 | tf_op jit(solution)/shard_map/while/body/eval_jaxpr/cond/branch_1_fun/dot_general | solution.py:44
  83.9 0.6 fusion.383
  85.2 4.5 %conditional.2 = (f32[1,256]{1,0:T(1,128)S(1)}) conditional(s32[]{:T(128)} %bitcast.447, () %tuple.436, (s32[1,256]{1,0:T(1,128)S(1)}, bf16[8,256,256]{1,2,0:T(8,128)(2,1)S(1)}, s32[]{:T(128)}, bf16[8,256]{1,0:T(8,128)(2,1)S(1)}, bf16[3,512,128]{2,1,0:T(8,128)(2,1)S(1)}, /*index=5*/bf16[3,128,512]{2,1,0:T(8,128)(2,1)S(1)}, f32[3,512]{1,0:T(4,128)S(1)}, ...), branch_computations={%region_4.4_spmd, %region_5.5_spmd} | conditional | flops 811698688 | bytes 8818188 | solution.py:152
  85.5 0.5 fusion.4
  86.0 0.5 fusion.6
  87.0 2.3 %fusion.10 = bf16[256,512]{1,0:T(8,128)(2,1)S(1)} fusion(bf16[1024,512]{1,0:T(8,128)(2,1)} %get-tuple-element.138, bf16[256,512]{0,1:T(8,128)(2,1)S(1)} %fusion.9, bf16[512,1024]{1,0:T(8,128)(2,1)} %get-tuple-element.136, f32[1024]{0:T(1024)S(1)} %get-tuple-element.137, f32[512]{0:T(512)S(1)} %get-tuple-element.139), kind=kOutput, calls=%fused_computation.15 | convolution fusion | flops 538050560 | bytes 2627584 | tf_op jit(solution)/shard_map/while/body/eval_jaxpr/cond/branch_1_fun/dot_general | solution.py:44
  89.7 0.6 fusion.383
  91.0 4.5 %conditional.2 = (f32[1,256]{1,0:T(1,128)S(1)}) conditional(s32[]{:T(128)} %bitcast.447, () %tuple.436, (s32[1,256]{1,0:T(1,128)S(1)}, bf16[8,256,256]{1,2,0:T(8,128)(2,1)S(1)}, s32[]{:T(128)}, bf16[8,256]{1,0:T(8,128)(2,1)S(1)}, bf16[3,512,128]{2,1,0:T(8,128)(2,1)S(1)}, /*index=5*/bf16[3,128,512]{2,1,0:T(8,128)(2,1)S(1)}, f32[3,512]{1,0:T(4,128)S(1)}, ...), branch_computations={%region_4.4_spmd, %region_5.5_spmd} | conditional | flops 811698688 | bytes 8818188 | solution.py:152
  91.4 0.5 fusion.4
  91.9 0.5 fusion.6
  92.9 2.3 %fusion.10 = bf16[256,512]{1,0:T(8,128)(2,1)S(1)} fusion(bf16[1024,512]{1,0:T(8,128)(2,1)} %get-tuple-element.138, bf16[256,512]{0,1:T(8,128)(2,1)S(1)} %fusion.9, bf16[512,1024]{1,0:T(8,128)(2,1)} %get-tuple-element.136, f32[1024]{0:T(1024)S(1)} %get-tuple-element.137, f32[512]{0:T(512)S(1)} %get-tuple-element.139), kind=kOutput, calls=%fused_computation.15 | convolution fusion | flops 538050560 | bytes 2627584 | tf_op jit(solution)/shard_map/while/body/eval_jaxpr/cond/branch_1_fun/dot_general | solution.py:44
  95.6 0.6 fusion.383
  96.9 4.5 %conditional.2 = (f32[1,256]{1,0:T(1,128)S(1)}) conditional(s32[]{:T(128)} %bitcast.447, () %tuple.436, (s32[1,256]{1,0:T(1,128)S(1)}, bf16[8,256,256]{1,2,0:T(8,128)(2,1)S(1)}, s32[]{:T(128)}, bf16[8,256]{1,0:T(8,128)(2,1)S(1)}, bf16[3,512,128]{2,1,0:T(8,128)(2,1)S(1)}, /*index=5*/bf16[3,128,512]{2,1,0:T(8,128)(2,1)S(1)}, f32[3,512]{1,0:T(4,128)S(1)}, ...), branch_computations={%region_4.4_spmd, %region_5.5_spmd} | conditional | flops 811698688 | bytes 8818188 | solution.py:152
  97.2 0.5 fusion.4
  97.7 0.5 fusion.6
  98.7 2.3 %fusion.10 = bf16[256,512]{1,0:T(8,128)(2,1)S(1)} fusion(bf16[1024,512]{1,0:T(8,128)(2,1)} %get-tuple-element.138, bf16[256,512]{0,1:T(8,128)(2,1)S(1)} %fusion.9, bf16[512,1024]{1,0:T(8,128)(2,1)} %get-tuple-element.136, f32[1024]{0:T(1024)S(1)} %get-tuple-element.137, f32[512]{0:T(512)S(1)} %get-tuple-element.139), kind=kOutput, calls=%fused_computation.15 | convolution fusion | flops 538050560 | bytes 2627584 | tf_op jit(solution)/shard_map/while/body/eval_jaxpr/cond/branch_1_fun/dot_general | solution.py:44
  101.4 0.6 fusion.383
  102.7 4.5 %conditional.2 = (f32[1,256]{1,0:T(1,128)S(1)}) conditional(s32[]{:T(128)} %bitcast.447, () %tuple.436, (s32[1,256]{1,0:T(1,128)S(1)}, bf16[8,256,256]{1,2,0:T(8,128)(2,1)S(1)}, s32[]{:T(128)}, bf16[8,256]{1,0:T(8,128)(2,1)S(1)}, bf16[3,512,128]{2,1,0:T(8,128)(2,1)S(1)}, /*index=5*/bf16[3,128,512]{2,1,0:T(8,128)(2,1)S(1)}, f32[3,512]{1,0:T(4,128)S(1)}, ...), branch_computations={%region_4.4_spmd, %region_5.5_spmd} | conditional | flops 811698688 | bytes 8818188 | solution.py:152
  103.1 0.5 fusion.4
  103.6 0.5 fusion.6
  104.6 2.3 %fusion.10 = bf16[256,512]{1,0:T(8,128)(2,1)S(1)} fusion(bf16[1024,512]{1,0:T(8,128)(2,1)} %get-tuple-element.138, bf16[256,512]{0,1:T(8,128)(2,1)S(1)} %fusion.9, bf16[512,1024]{1,0:T(8,128)(2,1)} %get-tuple-element.136, f32[1024]{0:T(1024)S(1)} %get-tuple-element.137, f32[512]{0:T(512)S(1)} %get-tuple-element.139), kind=kOutput, calls=%fused_computation.15 | convolution fusion | flops 538050560 | bytes 2627584 | tf_op jit(solution)/shard_map/while/body/eval_jaxpr/cond/branch_1_fun/dot_general | solution.py:44
  107.3 0.6 fusion.383
  108.6 4.5 %conditional.2 = (f32[1,256]{1,0:T(1,128)S(1)}) conditional(s32[]{:T(128)} %bitcast.447, () %tuple.436, (s32[1,256]{1,0:T(1,128)S(1)}, bf16[8,256,256]{1,2,0:T(8,128)(2,1)S(1)}, s32[]{:T(128)}, bf16[8,256]{1,0:T(8,128)(2,1)S(1)}, bf16[3,512,128]{2,1,0:T(8,128)(2,1)S(1)}, /*index=5*/bf16[3,128,512]{2,1,0:T(8,128)(2,1)S(1)}, f32[3,512]{1,0:T(4,128)S(1)}, ...), branch_computations={%region_4.4_spmd, %region_5.5_spmd} | conditional | flops 811698688 | bytes 8818188 | solution.py:152
  108.9 0.5 fusion.4
  109.4 0.5 fusion.6
  110.4 2.3 %fusion.10 = bf16[256,512]{1,0:T(8,128)(2,1)S(1)} fusion(bf16[1024,512]{1,0:T(8,128)(2,1)} %get-tuple-element.138, bf16[256,512]{0,1:T(8,128)(2,1)S(1)} %fusion.9, bf16[512,1024]{1,0:T(8,128)(2,1)} %get-tuple-element.136, f32[1024]{0:T(1024)S(1)} %get-tuple-element.137, f32[512]{0:T(512)S(1)} %get-tuple-element.139), kind=kOutput, calls=%fused_computation.15 | convolution fusion | flops 538050560 | bytes 2627584 | tf_op jit(solution)/shard_map/while/body/eval_jaxpr/cond/branch_1_fun/dot_general | solution.py:44
  113.1 0.6 fusion.383
  114.4 4.5 %conditional.2 = (f32[1,256]{1,0:T(1,128)S(1)}) conditional(s32[]{:T(128)} %bitcast.447, () %tuple.436, (s32[1,256]{1,0:T(1,128)S(1)}, bf16[8,256,256]{1,2,0:T(8,128)(2,1)S(1)}, s32[]{:T(128)}, bf16[8,256]{1,0:T(8,128)(2,1)S(1)}, bf16[3,512,128]{2,1,0:T(8,128)(2,1)S(1)}, /*index=5*/bf16[3,128,512]{2,1,0:T(8,128)(2,1)S(1)}, f32[3,512]{1,0:T(4,128)S(1)}, ...), branch_computations={%region_4.4_spmd, %region_5.5_spmd} | conditional | flops 811698688 | bytes 8818188 | solution.py:152
  114.8 0.5 fusion.4
  115.3 0.5 fusion.6
  116.2 2.3 %fusion.10 = bf16[256,512]{1,0:T(8,128)(2,1)S(1)} fusion(bf16[1024,512]{1,0:T(8,128)(2,1)} %get-tuple-element.138, bf16[256,512]{0,1:T(8,128)(2,1)S(1)} %fusion.9, bf16[512,1024]{1,0:T(8,128)(2,1)} %get-tuple-element.136, f32[1024]{0:T(1024)S(1)} %get-tuple-element.137, f32[512]{0:T(512)S(1)} %get-tuple-element.139), kind=kOutput, calls=%fused_computation.15 | convolution fusion | flops 538050560 | bytes 2627584 | tf_op jit(solution)/shard_map/while/body/eval_jaxpr/cond/branch_1_fun/dot_general | solution.py:44
  119.0 0.6 fusion.383
  120.3 4.5 %conditional.2 = (f32[1,256]{1,0:T(1,128)S(1)}) conditional(s32[]{:T(128)} %bitcast.447, () %tuple.436, (s32[1,256]{1,0:T(1,128)S(1)}, bf16[8,256,256]{1,2,0:T(8,128)(2,1)S(1)}, s32[]{:T(128)}, bf16[8,256]{1,0:T(8,128)(2,1)S(1)}, bf16[3,512,128]{2,1,0:T(8,128)(2,1)S(1)}, /*index=5*/bf16[3,128,512]{2,1,0:T(8,128)(2,1)S(1)}, f32[3,512]{1,0:T(4,128)S(1)}, ...), branch_computations={%region_4.4_spmd, %region_5.5_spmd} | conditional | flops 811698688 | bytes 8818188 | solution.py:152
  120.6 0.5 fusion.4
  121.1 0.5 fusion.6
  122.1 2.3 %fusion.10 = bf16[256,512]{1,0:T(8,128)(2,1)S(1)} fusion(bf16[1024,512]{1,0:T(8,128)(2,1)} %get-tuple-element.138, bf16[256,512]{0,1:T(8,128)(2,1)S(1)} %fusion.9, bf16[512,1024]{1,0:T(8,128)(2,1)} %get-tuple-element.136, f32[1024]{0:T(1024)S(1)} %get-tuple-element.137, f32[512]{0:T(512)S(1)} %get-tuple-element.139), kind=kOutput, calls=%fused_computation.15 | convolution fusion | flops 538050560 | bytes 2627584 | tf_op jit(solution)/shard_map/while/body/eval_jaxpr/cond/branch_1_fun/dot_general | solution.py:44
  124.8 0.6 reshape_reshape.3
  (428 shorter events, 33.6 us)
Async XLA Ops:
  0.0 28.9 %copy-start.4 = (bf16[8,128,256]{2,1,0:T(8,128)(2,1)S(1)}, bf16[8,128,256]{2,1,0:T(8,128)(2,1)}, u32[]{:S(2)}) copy-start(bf16[8,128,256]{2,1,0:T(8,128)(2,1)} %param.21) | copy-start | bytes 1572868
  50.6 18.4 %copy-start.2 = (bf16[1,1,2048,256]{3,2,1,0:T(8,128)(2,1)S(1)}, bf16[1,1,2048,256]{3,2,1,0:T(8,128)(2,1)}, u32[]{:S(2)}) copy-start(bf16[1,1,2048,256]{3,2,1,0:T(8,128)(2,1)} %param.24) | copy-start | bytes 3145732
  54.3 15.2 %copy-start.9 = (s32[1,1,8]{2,1,0:T(1,128)S(1)}, s32[1,1,8]{2,1,0:T(1,128)}, u32[]{:S(2)}) copy-start(s32[1,1,8]{2,1,0:T(1,128)} %param.25) | copy-start | bytes 100
  54.3 23.7 %copy-start = (bf16[3,512,128]{2,1,0:T(8,128)(2,1)S(1)}, bf16[3,512,128]{2,1,0:T(8,128)(2,1)}, u32[]{:S(2)}) copy-start(bf16[3,512,128]{2,1,0:T(8,128)(2,1)} %param.26) | copy-start | bytes 1179652
  54.3 23.7 %copy-start.1 = (bf16[3,128,512]{2,1,0:T(8,128)(2,1)S(1)}, bf16[3,128,512]{2,1,0:T(8,128)(2,1)}, u32[]{:S(2)}) copy-start(bf16[3,128,512]{2,1,0:T(8,128)(2,1)} %param.27) | copy-start | bytes 1179652
  54.3 23.7 %copy-start.3 = (f32[3,512]{1,0:T(4,128)S(1)}, f32[3,512]{1,0:T(4,128)}, u32[]{:S(2)}) copy-start(f32[3,512]{1,0:T(4,128)} %param.28) | copy-start | bytes 18436
  54.3 23.7 %copy-start.5 = (bf16[512,256]{1,0:T(8,128)(2,1)S(1)}, bf16[512,256]{1,0:T(8,128)(2,1)}, u32[]{:S(2)}) copy-start(bf16[512,256]{1,0:T(8,128)(2,1)} %param.33) | copy-start | bytes 786436
  54.3 23.7 %copy-start.6 = (f32[1024]{0:T(1024)S(1)}, f32[1024]{0:T(1024)}, u32[]{:S(2)}) copy-start(f32[1024]{0:T(1024)} %param.30) | copy-start | bytes 12292
  54.3 23.7 %copy-start.7 = (f32[512]{0:T(512)S(1)}, f32[512]{0:T(512)}, u32[]{:S(2)}) copy-start(f32[512]{0:T(512)} %param.32) | copy-start | bytes 6148
  54.4 23.7 %copy-start.8 = (f32[256]{0:T(256)S(1)}, f32[256]{0:T(256)}, u32[]{:S(2)}) copy-start(f32[256]{0:T(256)} %param.34) | copy-start | bytes 3076
  54.4 23.6 %copy-start.10 = (bf16[256]{0:T(256)(128)(2,1)S(1)}, bf16[256]{0:T(256)(128)(2,1)}, u32[]{:S(2)}) copy-start(bf16[256]{0:T(256)(128)(2,1)} %param.35) | copy-start | bytes 1540
  63.1 14.8 %all-to-all-start = ((bf16[8,8,1,8,256]{4,3,1,2,0:T(8,128)(2,1)}), bf16[8,8,1,8,256]{4,3,1,2,0:T(8,128)(2,1)S(1)}, u32[]{:S(2)}, u32[]{:S(2)}) async-start(bf16[8,8,1,8,256]{4,3,1,2,0:T(8,128)(2,1)} %constant_dynamic-update-slice_fusion), calls=%async_computation | async-start | bytes 524288 | tf_op jit(solution)/shard_map/all_to_all | solution.py:136
